TPU v7x, 512 devices: a whole 4x8x8 slice. The times are simulated.
512 devices in a mesh: mesh: 64 (over z, y), param: 8 (over x, core).
Axes of the slice: x: 4, y: 8, z: 8, core: 2. Of those that a mesh axis runs over, the one named last changes fastest.
Arguments:
- snapshots: bfloat16 [262144, 1024], P('mesh', 'param'), may hold values from -4 to 4
- coupling: bfloat16 [2048, 3, 128, 128], P('mesh'), may hold values from -0.3125 to 0.3125
- reaction_rate: float32 [1024], P('param'), may hold values from 0.1 to 1
- sketch: bfloat16 [256, 128], replicated, may hold values from -0.375 to 0.375
Outputs:
- mode_basis: bfloat16 [262144, 128], P('mesh', 'param')
All inputs are finite; a program needn't handle non-finite values.
Results may differ from a plain program's by a relative error of at most 0.0095.
Values may be sent and summed in bfloat16 or wider, within the bound.
No kernel may reach another device: no remote copies, remote signals or barrier semaphores. Data moves between devices by JAX's collectives and lax.ppermute only.
A program may use at most 64 MiB of HBM per device.

v0:
```python
import jax
import jax.numpy as jnp
from jax import lax
from jax.experimental import pallas as pl
from jax.experimental.pallas import tpu as pltpu
from jax.sharding import Mesh
from jax.sharding import PartitionSpec as P

SECTIONS = 3
BLOCK = 128
GROUP = ("mesh", "core")
PANEL = 16
F32 = jnp.float32
BF16 = jnp.bfloat16


def exchange(parts, axis):
    return lax.all_to_all(parts, axis, split_axis=0, concat_axis=0, tiled=True)


def copies_to(part, axis):
    return exchange(jnp.broadcast_to(part, (lax.axis_size(axis), *part.shape)), axis)


def three_parts(values):
    high = lax.reduce_precision(values, 8, 7)
    rest = values - high
    middle = lax.reduce_precision(rest, 8, 7)
    return jnp.stack([high, middle, rest - middle]).astype(BF16)


def dot(left, right, dims):
    return lax.dot_general(left, right, (dims, ((), ())), preferred_element_type=F32)


def terms_of(values, most):
    if values.dtype == BF16:
        return [values]
    terms = []
    for _ in range(most):
        terms.append(values.astype(BF16))
        values = values - terms[-1].astype(F32)
    return terms


def precise(left, right, dims, most=3):
    lefts, rights = terms_of(left, most), terms_of(right, most)
    pairs = [(i, j) for i in range(len(lefts)) for j in range(len(rights)) if i + j < most]
    return dot(
        jnp.concatenate([lefts[i] for i, _ in pairs], dims[0][0]),
        jnp.concatenate([rights[j] for _, j in pairs], dims[1][0]),
        dims,
    )


def stacked_rows(rows):
    sublane = lax.broadcasted_iota(jnp.int32, rows[0].shape, 0)
    eights = []
    for first in range(0, len(rows), 8):
        eight = rows[first]
        for i in range(1, 8):
            eight = jnp.where(sublane == i, rows[first + i], eight)
        eights.append(eight)
    return jnp.concatenate(eights, 0)


def eliminate(grams):
    size = grams[0].shape[0]
    shape = (8, size)
    lane = lax.broadcasted_iota(jnp.int32, (1, size), 1)
    row_of = lax.broadcasted_iota(jnp.int32, (size, size), 0)
    column_of = lax.broadcasted_iota(jnp.int32, (size, size), 1)
    unit = jnp.where(row_of == column_of, 1.0, 0.0).astype(F32)
    work = [(gram, unit) for gram in grams]
    done = [[] for _ in grams]
    scales = [jnp.zeros((1, size), F32) for _ in grams]
    for start in range(0, size, PANEL):
        following = []
        for index, (gram, inverse) in enumerate(work):
            value = {
                (i, j): jnp.broadcast_to(gram[i : i + 1, start + j : start + j + 1], shape)
                for i in range(PANEL)
                for j in range(i, PANEL)
            }
            rows = [jnp.broadcast_to(gram[i : i + 1], shape) for i in range(PANEL)]
            rows_inverse = [jnp.broadcast_to(inverse[i : i + 1], shape) for i in range(PANEL)]
            ratio = []
            for i in range(PANEL):
                inverse_pivot = 1.0 / value[i, i]
                ratio.append(inverse_pivot)
                scales[index] = jnp.where(lane == start + i, value[i, i][:1], scales[index])
                for j in range(i + 1, PANEL):
                    step = value[i, j] * inverse_pivot
                    for k in range(j, PANEL):
                        value[j, k] = value[j, k] - step * value[i, k]
                    rows[j] = rows[j] - step * rows[i]
                    rows_inverse[j] = rows_inverse[j] - step * rows_inverse[i]
            finished = stacked_rows(rows_inverse)
            done[index].append(finished)
            if start + PANEL < size:
                scaled = stacked_rows([row * by for row, by in zip(rows, ratio)])
                both = jnp.concatenate([stacked_rows(rows), finished], 1)
                update = precise(scaled, both, ((0,), (0,)))[start + PANEL :]
                following.append(
                    (gram[PANEL:] - update[:, :size], inverse[PANEL:] - update[:, size:])
                )
        work = following
    return [jnp.concatenate(parts, 0) for parts in done], scales


def sections_kernel(
    core_ref, rate_ref, snap, other, halo_own, halo_other, coupling, state_out, gram_out,
    first, second, blocks, sems,
):
    core = core_ref[0]
    away = 1 - core
    local = pl.multiple_of(384 * away, 128)
    beyond = pl.multiple_of(2432 * core, 128)
    copies = [
        (snap.at[pl.ds(pl.multiple_of(core * 1664, 128), 2432)], first.at[core, pl.ds(local, 2432)]),
        (other.at[pl.ds(0, 2432)], first.at[away, pl.ds(local, 2432)]),
        (halo_own.at[pl.ds(0, 384)], first.at[core, pl.ds(beyond, 384)]),
        (halo_other.at[pl.ds(0, 384)], first.at[away, pl.ds(beyond, 384)]),
        (coupling.at[pl.ds(core * 14 * 384, 18 * 384)], blocks.at[pl.ds(pl.multiple_of(away * 768, 128), 18 * 384)]),
        (halo_own.at[pl.ds(384, 384)], blocks.at[pl.ds(pl.multiple_of(core * 19 * 384, 128), 384)]),
        (halo_other.at[pl.ds(384, 384)], blocks.at[pl.ds(pl.multiple_of(384 + core * 17 * 384, 128), 384)]),
    ]
    started = [
        pltpu.make_async_copy(source, target, sems.at[i])
        for i, (source, target) in enumerate(copies)
    ]
    for copy in started:
        copy.start()
    for copy in started:
        copy.wait()
    rate = rate_ref[...]

    def section(source, number, store):
        def one(block, carry):
            at = pl.multiple_of(block * 128, 128)
            around = pl.multiple_of(at - 128, 128)
            matrix = pl.multiple_of((block - 1) * 384, 128)
            operator = jnp.concatenate(
                [
                    blocks[pl.ds(pl.multiple_of(matrix + 128, 128), 128)],
                    blocks[pl.ds(matrix, 128)],
                    blocks[pl.ds(pl.multiple_of(matrix + 256, 128), 128)],
                ],
                1,
            )
            window = jnp.concatenate(
                [source[0, pl.ds(around, 384)], source[1, pl.ds(around, 384)]], 1
            )
            mixed = jnp.dot(operator, window, preferred_element_type=F32)
            current = jnp.concatenate(
                [source[0, pl.ds(at, 128)], source[1, pl.ds(at, 128)]], 1
            ).astype(F32)
            new = (0.5 * current + 0.5 * mixed) / (1.0 + rate * current * current)
            store(block, new.astype(BF16))
            return carry

        lax.fori_loop(number, 22 - number, one, 0, unroll=True)

    def into(target):
        def store(block, value):
            at = pl.multiple_of(block * 128, 128)
            target[0, pl.ds(at, 128)] = value[:, :128]
            target[1, pl.ds(at, 128)] = value[:, 128:]

        return store

    def finish(block, value):
        state_out[pl.ds(pl.multiple_of((block - 3) * 128, 128), 128)] = value

    section(first, 1, into(second))
    section(second, 2, into(first))
    section(first, 3, finish)
    gram = jnp.zeros((256, 256), F32)
    for part in range(4):
        piece = state_out[part * 512 : part * 512 + 512]
        gram = gram + dot(piece, piece, ((0,), (0,)))
    gram_out[:256] = gram[:, :128]
    gram_out[256:] = gram[:, 128:]


def leaf_and_merge_kernel(gram_ref, sketch_ref, state_ref, basis_ref):
    gram = jnp.concatenate([gram_ref[:256], gram_ref[256:]], 1)
    sketch = sketch_ref[...]
    (lower, upper), _ = eliminate([gram[:128, :128], gram[128:, 128:]])
    mixing = jnp.concatenate(
        [precise(lower, sketch[:128], ((0,), (0,))), precise(upper, sketch[128:], ((0,), (0,)))], 0
    )
    merged_gram = precise(mixing, precise(gram, mixing, ((1,), (0,))), ((0,), (0,)))
    (merged,), (scale,) = eliminate([merged_gram])
    factor = jnp.concatenate(terms_of(precise(mixing, merged, ((1,), (1,)), 2), 2), 1)
    tail = jnp.concatenate([*terms_of(scale, 3), jnp.zeros((13, 128), BF16)], 0)
    for part in range(4):
        pieces = dot(state_ref[part * 512 : part * 512 + 512], factor, ((1,), (0,)))
        basis_ref[part, :512] = (pieces[:, :128] + pieces[:, 128:]).astype(BF16)
        basis_ref[part, 512:] = tail


PAIRS = ((0, 1), (2, 3), (0, 2), (0, 3), (1, 2), (1, 3))


def cross_kernel(bases_ref, cross_ref):
    for at, (i, j) in enumerate(PAIRS):
        cross_ref[at * 128 : at * 128 + 128] = dot(
            bases_ref[i, :512], bases_ref[j, :512], ((0,), (0,))
        )
    cross_ref[768:] = jnp.zeros((256, 128), F32)


def last_merges_kernel(cross_ref, sketch_ref, bases_ref, out_ref):
    sketch = sketch_ref[...]
    row_of = lax.broadcasted_iota(jnp.int32, (128, 128), 0)
    column_of = lax.broadcasted_iota(jnp.int32, (128, 128), 1)
    cross = [cross_ref[at * 128 : at * 128 + 128] for at in range(6)]
    scales = []
    for i in range(4):
        tail = bases_ref[i, 512:].astype(F32)
        scales.append(tail[0:1] + tail[1:2] + tail[2:3])

    def diagonal(scale):
        return jnp.where(row_of == column_of, jnp.broadcast_to(scale, (128, 128)), 0.0)

    def joined(first, second, between):
        gram = jnp.concatenate(
            [
                jnp.concatenate([diagonal(first), between], 1),
                jnp.concatenate([between.T, diagonal(second)], 1),
            ],
            0,
        )
        return precise(sketch, precise(gram, sketch, ((1,), (0,))), ((0,), (0,)))

    pair_grams = [joined(scales[0], scales[1], cross[0]), joined(scales[2], scales[3], cross[1])]
    (low, high), (low_scale, high_scale) = eliminate(pair_grams)
    low = precise(sketch, low, ((1,), (1,)))
    high = precise(sketch, high, ((1,), (1,)))
    between = jnp.concatenate(
        [jnp.concatenate([cross[2], cross[3]], 1), jnp.concatenate([cross[4], cross[5]], 1)], 0
    )
    between = precise(low, precise(between, high, ((1,), (0,))), ((0,), (0,)))
    (root,), _ = eliminate([joined(low_scale, high_scale, between)])
    mixed = precise(sketch, root, ((1,), (1,)), 2)
    weights = jnp.concatenate(
        [
            precise(low, mixed[:128], ((1,), (0,)), 2),
            precise(high, mixed[128:], ((1,), (0,)), 2),
        ],
        0,
    )
    weights = jnp.concatenate(terms_of(weights, 2), 1)
    pieces = dot(jnp.concatenate([bases_ref[i, :512] for i in range(4)], 1), weights, ((1,), (0,)))
    out_ref[...] = (pieces[:, :128] + pieces[:, 128:]).T.astype(BF16)


def call(kernel, out_shape, **options):
    return pl.pallas_call(kernel, out_shape=out_shape, **options)


def on_device(snapshots, coupling, reaction_rate, sketch):
    core = lax.axis_index("core")
    away = 1 - core
    slabs = lax.axis_size("mesh")
    operators = coupling.reshape(-1, BLOCK)

    tail = jnp.pad(three_parts(reaction_rate), ((0, 13), (0, 0)))
    wanted = lax.dynamic_slice_in_dim(snapshots, away * 1664, 2432, 0)
    other = lax.ppermute(jnp.concatenate([wanted, tail], 0), "core", [(0, 1), (1, 0)])

    def edge(above, block):
        states = lax.dynamic_slice_in_dim(snapshots, above * 3712, 384, 0)
        return jnp.concatenate([states, lax.dynamic_slice_in_dim(operators, block * 384, 384, 0)], 0)

    same, crossed = [], []
    for slab in range(slabs - 1):
        same += [(2 * slab, 2 * slab + 2), (2 * slab + 3, 2 * slab + 1)]
        crossed += [(2 * slab + 1, 2 * slab + 2), (2 * slab + 2, 2 * slab + 1)]
    halo_own = lax.ppermute(edge(away, 1 + 29 * away), GROUP, same)
    halo_other = lax.ppermute(edge(core, 31 * core), GROUP, crossed)

    other_rate = other[2432:2435].astype(F32).sum(0)
    rates = jnp.where(
        core == 0,
        jnp.concatenate([reaction_rate, other_rate]),
        jnp.concatenate([other_rate, reaction_rate]),
    )[None]
    hbm = pl.BlockSpec(memory_space=pl.ANY)
    vmem = pl.BlockSpec(memory_space=pltpu.VMEM)
    state, gram = call(
        sections_kernel,
        (jax.ShapeDtypeStruct((2048, 256), BF16), jax.ShapeDtypeStruct((512, 128), F32)),
        in_specs=[pl.BlockSpec(memory_space=pltpu.SMEM), vmem, hbm, hbm, hbm, hbm, hbm],
        out_specs=(vmem, vmem),
        scratch_shapes=[
            pltpu.VMEM((2, 2816, 128), BF16),
            pltpu.VMEM((2, 2816, 128), BF16),
            pltpu.VMEM((7680, 128), BF16),
            pltpu.SemaphoreType.DMA((7,)),
        ],
        name="sections",
    )(core[None].astype(jnp.int32), rates, snapshots, other, halo_own, halo_other, operators)

    own = exchange(gram.reshape(128, 4, 128), GROUP).sum(0)
    gram = copies_to(own, GROUP).reshape(512, 128)
    bases = call(
        leaf_and_merge_kernel, jax.ShapeDtypeStruct((4, 528, 128), BF16), name="leaf_and_merge"
    )(gram, sketch, state)
    bases = exchange(bases, "x")
    cross = call(cross_kernel, jax.ShapeDtypeStruct((1024, 128), F32), name="cross")(bases)
    own = exchange(cross.reshape(128, 8, 128), GROUP).sum(0)
    own = copies_to(own, "x").sum(0)
    cross = copies_to(own, GROUP).reshape(1024, 128)
    turned = call(
        last_merges_kernel, jax.ShapeDtypeStruct((128, 512), BF16), name="last_merges"
    )(cross, sketch, bases)
    turned = exchange(turned.reshape(8, 16, 512), ("x", "core"))
    return turned.reshape(4, 2, 16, 512).transpose(1, 0, 3, 2).reshape(4096, 16)


def solution(mesh):
    fine = Mesh(mesh.devices.reshape(mesh.devices.shape[0], -1, 2), ("mesh", "x", "core"))
    param = ("x", "core")
    return jax.shard_map(
        on_device,
        mesh=fine,
        in_specs=(P("mesh", param), P("mesh", None, None, None), P(param), P()),
        out_specs=P("mesh", param),
        check_vma=False,
    )
```

profile of v0, /device:TPU:1, one launch (start us, length us, event | category | flops | bytes accessed | tf_op | source)
XLA Modules:
  0.0 195.4 jit_solution(5698053948911797262)
XLA Ops:
  0.0 0.7 fusion.5
  0.7 1.1 constant_dynamic-slice_fusion.4
  1.8 0.0 copy-start.3
  1.9 8.7 %collective-permute-start = (bf16[2448,128]{1,0:T(8,128)(2,1)S(1)}, bf16[2448,128]{1,0:T(8,128)(2,1)S(1)}, u32[]{:S(2)}, u32[]{:S(2)}) collective-permute-start(bf16[2448,128]{1,0:T(8,128)(2,1)S(1)} %pad_maximum_fusion), channel_id=1, source_target_pairs={{0,1},{1,0},{2,3},{3,2},{4,5},{5,4},{6,7},{7,6},{8,9},{9,8},{10,11... | collective-permute-start | bytes 1880072 | tf_op jit(solution)/shard_map/ppermute | solution.py:271
  10.6 1.0 constant_dynamic-slice_fusion.1
  11.6 1.0 constant_dynamic-slice_fusion
  12.6 1.3 collective-permute-start.1
  13.9 1.9 collective-permute-start.2
  15.8 0.0 collective-permute-done.other
  15.8 0.0 copy-start
  15.9 0.0 copy-done.3
  15.9 0.6 broadcast_select_fusion.rate_ref
  16.5 2.7 %collective-permute-done.1.halo_own = bf16[768,128]{1,0:T(8,128)(2,1)S(1)} collective-permute-done((bf16[768,128]{1,0:T(8,128)(2,1)S(1)}, bf16[768,128]{1,0:T(8,128)(2,1)S(1)}, u32[]{:S(2)}, u32[]{:S(2)}) %collective-permute-start.1) | collective-permute-done | bytes 196640 | tf_op jit(solution)/shard_map/ppermute | solution.py:281
  19.2 0.0 copy-start.1
  19.2 1.9 collective-permute-done.2.halo_other
  21.1 0.0 copy-start.2
  21.1 0.0 copy-done
  21.1 0.0 copy-done.1
  21.1 0.7 copy-done.2
  21.8 6.2 %sections.1 = (bf16[2048,256]{1,0:T(8,128)(2,1)}, f32[512,128]{1,0:T(8,128)}) custom-call(s32[1]{0:T(128)} %bitcast.core_ref, f32[1,256]{1,0:T(1,128)} %broadcast_select_fusion.rate_ref, bf16[4096,128]{1,0:T(8,128)(2,1)} %snap.1, bf16[2448,128]{1,0:T(8,128)(2,1)} %copy-done, bf16[768,128]{1,0:T(8,128)(2,1)} %copy-done.1, bf16[768,128]{1,0:T(8,128)(2,1)} %copy-done.2, ...), custom_call_target="tpu_custom_call" | custom-call | tf_op jit(solution)/shard_map/sections/pallas_call | solution.py:292
  28.0 29.2 %all_to_all.35 = f32[128,4,128]{2,1,0:T(4,128)S(1)} all-to-all(f32[128,4,128]{2,1,0:T(4,128)} %bitcast.29), channel_id=1, replica_groups=mesh['mesh'=64,'x'=4,'core'=2] {'mesh','core'}, dimensions={0} | all-to-all | bytes 524288 | tf_op jit(solution)/shard_map/all_to_all | solution.py:18
  57.2 0.1 reduce_sum.37
  57.4 20.9 %all_to_all.36 = f32[128,4,128]{2,1,0:T(4,128)} all-to-all(f32[128,4,128]{2,1,0:T(4,128)S(1)} %broadcast_in_dim.14), channel_id=1, replica_groups=mesh['mesh'=64,'x'=4,'core'=2] {'mesh','core'}, dimensions={0} | all-to-all | bytes 524288 | tf_op jit(solution)/shard_map/all_to_all | solution.py:18
  78.3 14.7 %leaf_and_merge.1 = bf16[4,528,128]{2,1,0:T(8,128)(2,1)} custom-call(f32[512,128]{1,0:T(8,128)} %bitcast.25, bf16[256,128]{1,0:T(8,128)(2,1)} %sketch_ref.3, bf16[2048,256]{1,0:T(8,128)(2,1)} %get-tuple-element.8.state_ref), custom_call_target="tpu_custom_call" | custom-call | tf_op jit(solution)/shard_map/leaf_and_merge/pallas_call | solution.py:308
  93.0 13.4 %all_to_all.37.bases_ref = bf16[4,528,128]{2,1,0:T(8,128)(2,1)} all-to-all(bf16[4,528,128]{2,1,0:T(8,128)(2,1)} %leaf_and_merge.1), channel_id=1, replica_groups=mesh['mesh'=64,'x'=4,'core'=2] {'x'}, dimensions={0} | all-to-all | bytes 1081344 | tf_op jit(solution)/shard_map/all_to_all | solution.py:18
  106.4 2.3 %cross.1 = f32[1024,128]{1,0:T(8,128)} custom-call(bf16[4,528,128]{2,1,0:T(8,128)(2,1)} %all_to_all.37.bases_ref), custom_call_target="tpu_custom_call" | custom-call | tf_op jit(solution)/shard_map/cross/pallas_call | solution.py:312
  108.7 27.5 %all_to_all.38 = f32[128,8,128]{2,1,0:T(8,128)S(1)} all-to-all(f32[128,8,128]{2,1,0:T(8,128)} %bitcast.24), channel_id=1, replica_groups=mesh['mesh'=64,'x'=4,'core'=2] {'mesh','core'}, dimensions={0} | all-to-all | bytes 1048576 | tf_op jit(solution)/shard_map/all_to_all | solution.py:18
  136.1 0.1 reduce_sum.38
  136.3 6.6 %all_to_all.39 = f32[4,8,128]{2,1,0:T(8,128)S(1)} all-to-all(f32[4,8,128]{2,1,0:T(8,128)S(1)} %broadcast_in_dim.15), channel_id=1, replica_groups=mesh['mesh'=64,'x'=4,'core'=2] {'x'}, dimensions={0} | all-to-all | bytes 32768 | tf_op jit(solution)/shard_map/all_to_all | solution.py:18
  142.9 27.0 %all_to_all.40 = f32[128,8,128]{2,1,0:T(8,128)} all-to-all(f32[128,8,128]{2,1,0:T(8,128)S(1)} %broadcast_in_dim.16), channel_id=1, replica_groups=mesh['mesh'=64,'x'=4,'core'=2] {'mesh','core'}, dimensions={0} | all-to-all | bytes 1048576 | tf_op jit(solution)/shard_map/all_to_all | solution.py:18
  169.9 16.4 %last_merges.1 = bf16[128,512]{1,0:T(8,128)(2,1)} custom-call(f32[1024,128]{1,0:T(8,128)} %bitcast.23, bf16[256,128]{1,0:T(8,128)(2,1)} %sketch_ref.3, bf16[4,528,128]{2,1,0:T(8,128)(2,1)} %all_to_all.37.bases_ref), custom_call_target="tpu_custom_call" | custom-call | tf_op jit(solution)/shard_map/last_merges/pallas_call | solution.py:316
  186.3 8.3 %all_to_all.41 = bf16[8,16,512]{2,1,0:T(8,128)(2,1)S(1)} all-to-all(bf16[8,16,512]{2,1,0:T(8,128)(2,1)} %bitcast.26), channel_id=1, replica_groups=mesh['mesh'=64,'x'=4,'core'=2] {'x','core'}, dimensions={0} | all-to-all | bytes 262144 | tf_op jit(solution)/shard_map/all_to_all | solution.py:18
  194.5 0.1 copy.8
  194.6 0.7 reshape.86
  (9 shorter events, 0.2 us)
Async XLA Ops:
  1.8 14.1 %copy-start.3 = (f32[128]{0:T(128)S(1)}, f32[128]{0:T(128)}, u32[]{:S(2)}) copy-start(f32[128]{0:T(128)} %param.6) | copy-start | bytes 1540
  1.9 14.0 %collective-permute-start = (bf16[2448,128]{1,0:T(8,128)(2,1)S(1)}, bf16[2448,128]{1,0:T(8,128)(2,1)S(1)}, u32[]{:S(2)}, u32[]{:S(2)}) collective-permute-start(bf16[2448,128]{1,0:T(8,128)(2,1)S(1)} %pad_maximum_fusion), channel_id=1, source_target_pairs={{0,1},{1,0},{2,3},{3,2},{4,5},{5,4},{6,7},{7,6},{8,9},{9,8},{10,11... | collective-permute-start | bytes 1880072 | tf_op jit(solution)/shard_map/ppermute | solution.py:271
  12.6 6.6 %collective-permute-start.1 = (bf16[768,128]{1,0:T(8,128)(2,1)S(1)}, bf16[768,128]{1,0:T(8,128)(2,1)S(1)}, u32[]{:S(2)}, u32[]{:S(2)}) collective-permute-start(bf16[768,128]{1,0:T(8,128)(2,1)S(1)} %pad_maximum_fusion.1), channel_id=1, source_target_pairs={{0,8},{9,1},{8,16},{17,9},{16,24},{25,17},{24,32},{33,25},{32,40},... | collective-permute-start | bytes 589832 | tf_op jit(solution)/shard_map/ppermute | solution.py:281
  13.9 7.2 %collective-permute-start.2 = (bf16[768,128]{1,0:T(8,128)(2,1)S(1)}, bf16[768,128]{1,0:T(8,128)(2,1)S(1)}, u32[]{:S(2)}, u32[]{:S(2)}) collective-permute-start(bf16[768,128]{1,0:T(8,128)(2,1)S(1)} %pad_maximum_fusion.2), channel_id=1, source_target_pairs={{1,8},{8,1},{9,16},{16,9},{17,24},{24,17},{25,32},{32,25},{33,40},... | collective-permute-start | bytes 589832 | tf_op jit(solution)/shard_map/ppermute | solution.py:282
  15.8 5.3 %copy-start = (bf16[2448,128]{1,0:T(8,128)(2,1)}, bf16[2448,128]{1,0:T(8,128)(2,1)S(1)}, u32[]{:S(2)}) copy-start(bf16[2448,128]{1,0:T(8,128)(2,1)S(1)} %collective-permute-done.other) | copy-start | bytes 1880068
  19.2 1.9 copy-start.1
  21.1 0.7 copy-start.2
where the time goes:
time: 196 us; the launch traced here: 195 us
  blocking collectives  133 us (68%)
  Pallas kernels  39.6 us (20%)
  starting transfers between devices  12 us (6%)
  local copies, waits for them, and re-layouts  4.65 us (2%)
  waiting for transfers between devices  4.59 us (2%)
    all_to_all x7, blocking collectives, exchange(): return lax.all_to_all(parts, axis, split_axis=0, concat_axis=0, tiled=True)  133 us
    pallas_call x1, Pallas kernels, on_device(): call(last_merges_kernel, jax.ShapeDtypeStruct((128, 512), BF16), name='la...  16.4 us
    pallas_call x1, Pallas kernels, on_device(): call(leaf_and_merge_kernel, jax.ShapeDtypeStruct((4, 528, 128), BF16), na...  14.7 us
    ppermute x1, starting transfers between devices, on_device(): lax.ppermute(jnp.concatenate([wanted, tail], 0), 'core', [(0, 1), (1, 0)])  8.75 us
    pallas_call x1, Pallas kernels, on_device(): call(sections_kernel, (jax.ShapeDtypeStruct((2048, 256), BF16), jax.Shape...  6.22 us
  transfers between devices with their start and end apart: 3, of which 2 were waited for; matrix products, arithmetic and copies ran while one was open for 1% of the time, Pallas kernels for 0%

commit v1 on v0

--- a/solution.py
+++ b/solution.py
@@ -9,6 +9,7 @@
 SECTIONS = 3
 BLOCK = 128
 GROUP = ("mesh", "core")
+PARAM = ("x", "core")
 PANEL = 16
 F32 = jnp.float32
 BF16 = jnp.bfloat16
@@ -20,13 +21,6 @@
 
 def copies_to(part, axis):
     return exchange(jnp.broadcast_to(part, (lax.axis_size(axis), *part.shape)), axis)
-
-
-def three_parts(values):
-    high = lax.reduce_precision(values, 8, 7)
-    rest = values - high
-    middle = lax.reduce_precision(rest, 8, 7)
-    return jnp.stack([high, middle, rest - middle]).astype(BF16)
 
 
 def dot(left, right, dims):
@@ -108,6 +102,27 @@
     return [jnp.concatenate(parts, 0) for parts in done], scales
 
 
+def pack_kernel(core_ref, rate_ref, snap, coupling, wanted, edge_own, edge_other, sems):
+    core = core_ref[0]
+    away = 1 - core
+    sources = [
+        (snap.at[pl.ds(pl.multiple_of(away * 3712, 128), 384)], edge_own.at[pl.ds(0, 384)]),
+        (coupling.at[pl.ds(pl.multiple_of(384 + 29 * 384 * away, 128), 384)], edge_own.at[pl.ds(384, 384)]),
+        (snap.at[pl.ds(pl.multiple_of(core * 3712, 128), 384)], edge_other.at[pl.ds(0, 384)]),
+        (coupling.at[pl.ds(pl.multiple_of(31 * 384 * core, 128), 384)], edge_other.at[pl.ds(384, 384)]),
+        (snap.at[pl.ds(pl.multiple_of(away * 1664, 128), 2432)], wanted.at[pl.ds(0, 2432)]),
+    ]
+    copies = [pltpu.make_async_copy(*ends, sems.at[i]) for i, ends in enumerate(sources)]
+    for copy in copies:
+        copy.start()
+    wanted[2432:] = jnp.concatenate([*terms_of(rate_ref[...], 3), jnp.zeros((13, 128), BF16)], 0)
+    for copy in copies:
+        copy.wait()
+
+
+CHUNKS = (0, 5, 10, 14, 18)
+
+
 def sections_kernel(
     core_ref, rate_ref, snap, other, halo_own, halo_other, coupling, state_out, gram_out,
     first, second, blocks, sems,
@@ -116,61 +131,65 @@
     away = 1 - core
     local = pl.multiple_of(384 * away, 128)
     beyond = pl.multiple_of(2432 * core, 128)
-    copies = [
+    sources = [
         (snap.at[pl.ds(pl.multiple_of(core * 1664, 128), 2432)], first.at[core, pl.ds(local, 2432)]),
         (other.at[pl.ds(0, 2432)], first.at[away, pl.ds(local, 2432)]),
         (halo_own.at[pl.ds(0, 384)], first.at[core, pl.ds(beyond, 384)]),
         (halo_other.at[pl.ds(0, 384)], first.at[away, pl.ds(beyond, 384)]),
-        (coupling.at[pl.ds(core * 14 * 384, 18 * 384)], blocks.at[pl.ds(pl.multiple_of(away * 768, 128), 18 * 384)]),
         (halo_own.at[pl.ds(384, 384)], blocks.at[pl.ds(pl.multiple_of(core * 19 * 384, 128), 384)]),
         (halo_other.at[pl.ds(384, 384)], blocks.at[pl.ds(pl.multiple_of(384 + core * 17 * 384, 128), 384)]),
     ]
-    started = [
-        pltpu.make_async_copy(source, target, sems.at[i])
-        for i, (source, target) in enumerate(copies)
-    ]
-    for copy in started:
+    for begin, end in zip(CHUNKS, CHUNKS[1:]):
+        sources.append(
+            (
+                coupling.at[pl.ds(pl.multiple_of((core * 14 + begin) * 384, 128), (end - begin) * 384)],
+                blocks.at[pl.ds(pl.multiple_of(away * 768 + begin * 384, 128), (end - begin) * 384)],
+            )
+        )
+    copies = [pltpu.make_async_copy(*ends, sems.at[i]) for i, ends in enumerate(sources)]
+    for copy in copies:
         copy.start()
-    for copy in started:
+    for copy in copies[:6]:
         copy.wait()
-    rate = rate_ref[...]
+    own_rate = rate_ref[...]
+    tail = other[2432:].astype(F32)
+    other_rate = tail[0:1] + tail[1:2] + tail[2:3]
+    even = jnp.full((1, 128), core, jnp.int32) == 0
+    rate = jnp.concatenate(
+        [jnp.where(even, own_rate, other_rate), jnp.where(even, other_rate, own_rate)], 1
+    )
 
     def section(source, number, store):
-        def one(block, carry):
-            at = pl.multiple_of(block * 128, 128)
-            around = pl.multiple_of(at - 128, 128)
-            matrix = pl.multiple_of((block - 1) * 384, 128)
+        for block in range(number, 22 - number):
+            if number == 1 and block - 1 in CHUNKS[:-1]:
+                copies[6 + CHUNKS.index(block - 1)].wait()
+            at = block * 128
+            matrix = (block - 1) * 384
             operator = jnp.concatenate(
                 [
-                    blocks[pl.ds(pl.multiple_of(matrix + 128, 128), 128)],
-                    blocks[pl.ds(matrix, 128)],
-                    blocks[pl.ds(pl.multiple_of(matrix + 256, 128), 128)],
+                    blocks[matrix + 128 : matrix + 256],
+                    blocks[matrix : matrix + 128],
+                    blocks[matrix + 256 : matrix + 384],
                 ],
                 1,
             )
             window = jnp.concatenate(
-                [source[0, pl.ds(around, 384)], source[1, pl.ds(around, 384)]], 1
+                [source[0, at - 128 : at + 256], source[1, at - 128 : at + 256]], 1
             )
             mixed = jnp.dot(operator, window, preferred_element_type=F32)
-            current = jnp.concatenate(
-                [source[0, pl.ds(at, 128)], source[1, pl.ds(at, 128)]], 1
-            ).astype(F32)
+            current = window[128:256].astype(F32)
             new = (0.5 * current + 0.5 * mixed) / (1.0 + rate * current * current)
             store(block, new.astype(BF16))
-            return carry
-
-        lax.fori_loop(number, 22 - number, one, 0, unroll=True)
 
     def into(target):
         def store(block, value):
-            at = pl.multiple_of(block * 128, 128)
-            target[0, pl.ds(at, 128)] = value[:, :128]
-            target[1, pl.ds(at, 128)] = value[:, 128:]
+            target[0, block * 128 : block * 128 + 128] = value[:, :128]
+            target[1, block * 128 : block * 128 + 128] = value[:, 128:]
 
         return store
 
     def finish(block, value):
-        state_out[pl.ds(pl.multiple_of((block - 3) * 128, 128), 128)] = value
+        state_out[(block - 3) * 128 : (block - 2) * 128] = value
 
     section(first, 1, into(second))
     section(second, 2, into(first))
@@ -208,7 +227,6 @@
         cross_ref[at * 128 : at * 128 + 128] = dot(
             bases_ref[i, :512], bases_ref[j, :512], ((0,), (0,))
         )
-    cross_ref[768:] = jnp.zeros((256, 128), F32)
 
 
 def last_merges_kernel(cross_ref, sketch_ref, bases_ref, out_ref):
@@ -234,99 +252,98 @@
         )
         return precise(sketch, precise(gram, sketch, ((1,), (0,))), ((0,), (0,)))
 
+    between = jnp.concatenate(
+        [jnp.concatenate([cross[2], cross[3]], 1), jnp.concatenate([cross[4], cross[5]], 1)], 0
+    )
+    between = precise(sketch, precise(between, sketch, ((1,), (0,))), ((0,), (0,)))
     pair_grams = [joined(scales[0], scales[1], cross[0]), joined(scales[2], scales[3], cross[1])]
     (low, high), (low_scale, high_scale) = eliminate(pair_grams)
-    low = precise(sketch, low, ((1,), (1,)))
-    high = precise(sketch, high, ((1,), (1,)))
-    between = jnp.concatenate(
-        [jnp.concatenate([cross[2], cross[3]], 1), jnp.concatenate([cross[4], cross[5]], 1)], 0
-    )
-    between = precise(low, precise(between, high, ((1,), (0,))), ((0,), (0,)))
-    (root,), _ = eliminate([joined(low_scale, high_scale, between)])
-    mixed = precise(sketch, root, ((1,), (1,)), 2)
+    between = precise(low, precise(between, high, ((1,), (1,))), ((1,), (0,)))
+    root_gram = joined(low_scale, high_scale, between)
     weights = jnp.concatenate(
         [
-            precise(low, mixed[:128], ((1,), (0,)), 2),
-            precise(high, mixed[128:], ((1,), (0,)), 2),
+            precise(sketch, precise(low, sketch[:128], ((0,), (0,))), ((1,), (0,)), 2),
+            precise(sketch, precise(high, sketch[128:], ((0,), (0,))), ((1,), (0,)), 2),
         ],
         0,
     )
-    weights = jnp.concatenate(terms_of(weights, 2), 1)
+    (root,), _ = eliminate([root_gram])
+    weights = jnp.concatenate(terms_of(precise(weights, root, ((1,), (1,)), 2), 2), 1)
     pieces = dot(jnp.concatenate([bases_ref[i, :512] for i in range(4)], 1), weights, ((1,), (0,)))
     out_ref[...] = (pieces[:, :128] + pieces[:, 128:]).T.astype(BF16)
 
 
+def on_chip(values):
+    return pltpu.with_memory_space_constraint(values, pltpu.VMEM)
+
+
 def call(kernel, out_shape, **options):
     return pl.pallas_call(kernel, out_shape=out_shape, **options)
 
 
 def on_device(snapshots, coupling, reaction_rate, sketch):
     core = lax.axis_index("core")
-    away = 1 - core
     slabs = lax.axis_size("mesh")
     operators = coupling.reshape(-1, BLOCK)
-
-    tail = jnp.pad(three_parts(reaction_rate), ((0, 13), (0, 0)))
-    wanted = lax.dynamic_slice_in_dim(snapshots, away * 1664, 2432, 0)
-    other = lax.ppermute(jnp.concatenate([wanted, tail], 0), "core", [(0, 1), (1, 0)])
-
-    def edge(above, block):
-        states = lax.dynamic_slice_in_dim(snapshots, above * 3712, 384, 0)
-        return jnp.concatenate([states, lax.dynamic_slice_in_dim(operators, block * 384, 384, 0)], 0)
 
     same, crossed = [], []
     for slab in range(slabs - 1):
         same += [(2 * slab, 2 * slab + 2), (2 * slab + 3, 2 * slab + 1)]
         crossed += [(2 * slab + 1, 2 * slab + 2), (2 * slab + 2, 2 * slab + 1)]
-    halo_own = lax.ppermute(edge(away, 1 + 29 * away), GROUP, same)
-    halo_other = lax.ppermute(edge(core, 31 * core), GROUP, crossed)
-
-    other_rate = other[2432:2435].astype(F32).sum(0)
-    rates = jnp.where(
-        core == 0,
-        jnp.concatenate([reaction_rate, other_rate]),
-        jnp.concatenate([other_rate, reaction_rate]),
-    )[None]
     hbm = pl.BlockSpec(memory_space=pl.ANY)
     vmem = pl.BlockSpec(memory_space=pltpu.VMEM)
+    smem = pl.BlockSpec(memory_space=pltpu.SMEM)
+    place = core[None].astype(jnp.int32)
+    rate = reaction_rate[None]
+    wanted, edge_own, edge_other = call(
+        pack_kernel,
+        (pltpu.VMEM((2448, 128), BF16), pltpu.VMEM((768, 128), BF16), pltpu.VMEM((768, 128), BF16)),
+        in_specs=[smem, vmem, hbm, hbm],
+        out_specs=(vmem, vmem, vmem),
+        scratch_shapes=[pltpu.SemaphoreType.DMA((5,))],
+        name="pack",
+    )(place, rate, snapshots, operators)
+    halo_own = lax.ppermute(edge_own, GROUP, same)
+    halo_other = lax.ppermute(edge_other, GROUP, crossed)
+    other = lax.ppermute(wanted, "core", [(0, 1), (1, 0)])
     state, gram = call(
         sections_kernel,
-        (jax.ShapeDtypeStruct((2048, 256), BF16), jax.ShapeDtypeStruct((512, 128), F32)),
-        in_specs=[pl.BlockSpec(memory_space=pltpu.SMEM), vmem, hbm, hbm, hbm, hbm, hbm],
+        (pltpu.VMEM((2048, 256), BF16), pltpu.VMEM((512, 128), F32)),
+        in_specs=[smem, vmem, hbm, vmem, vmem, vmem, hbm],
         out_specs=(vmem, vmem),
         scratch_shapes=[
             pltpu.VMEM((2, 2816, 128), BF16),
             pltpu.VMEM((2, 2816, 128), BF16),
             pltpu.VMEM((7680, 128), BF16),
-            pltpu.SemaphoreType.DMA((7,)),
+            pltpu.SemaphoreType.DMA((10,)),
         ],
         name="sections",
-    )(core[None].astype(jnp.int32), rates, snapshots, other, halo_own, halo_other, operators)
+    )(place, rate, snapshots, on_chip(other), on_chip(halo_own), on_chip(halo_other), operators)
 
     own = exchange(gram.reshape(128, 4, 128), GROUP).sum(0)
     gram = copies_to(own, GROUP).reshape(512, 128)
     bases = call(
-        leaf_and_merge_kernel, jax.ShapeDtypeStruct((4, 528, 128), BF16), name="leaf_and_merge"
-    )(gram, sketch, state)
-    bases = exchange(bases, "x")
-    cross = call(cross_kernel, jax.ShapeDtypeStruct((1024, 128), F32), name="cross")(bases)
-    own = exchange(cross.reshape(128, 8, 128), GROUP).sum(0)
-    own = copies_to(own, "x").sum(0)
-    cross = copies_to(own, GROUP).reshape(1024, 128)
+        leaf_and_merge_kernel, pltpu.VMEM((4, 528, 128), BF16), name="leaf_and_merge"
+    )(on_chip(gram), sketch, on_chip(state))
+    bases = on_chip(exchange(bases, "x"))
+    cross = call(cross_kernel, pltpu.VMEM((768, 128), F32), name="cross")(bases)
+    own = exchange(cross.reshape(8, 96, 128), PARAM).sum(0)
+    own = jnp.pad(own, ((0, 32), (0, 0)))
+    own = copies_to(exchange(own.reshape(64, 2, 128), "mesh").sum(0), "mesh")
+    cross = copies_to(own.reshape(128, 128)[:96], PARAM).reshape(768, 128)
     turned = call(
-        last_merges_kernel, jax.ShapeDtypeStruct((128, 512), BF16), name="last_merges"
-    )(cross, sketch, bases)
-    turned = exchange(turned.reshape(8, 16, 512), ("x", "core"))
+        last_merges_kernel, pltpu.VMEM((128, 512), BF16), name="last_merges"
+    )(on_chip(cross), sketch, bases)
+    turned = exchange(turned.reshape(8, 16, 512), PARAM)
     return turned.reshape(4, 2, 16, 512).transpose(1, 0, 3, 2).reshape(4096, 16)
 
 
 def solution(mesh):
     fine = Mesh(mesh.devices.reshape(mesh.devices.shape[0], -1, 2), ("mesh", "x", "core"))
-    param = ("x", "core")
     return jax.shard_map(
         on_device,
         mesh=fine,
-        in_specs=(P("mesh", param), P("mesh", None, None, None), P(param), P()),
-        out_specs=P("mesh", param),
+        in_specs=(P("mesh", PARAM), P("mesh", None, None, None), P(PARAM), P()),
+        out_specs=P("mesh", PARAM),
         check_vma=False,
     )

time: 196 us -> 182 us (0.929)
  blocking collectives: 133 us -> 126 us
  local copies, waits for them, and re-layouts: 4.65 us -> 0.93 us
  Pallas kernels: 39.6 us -> 36.7 us
    all_to_all x7 -> x8, blocking collectives: 133 us -> 126 us  [exchange(): return lax.all_to_all(parts, axis, split_axis=0, concat_axis=0, tiled=True)]
    dynamic_slice x3 -> x0, local copies, waits for them, and re-layouts: 3.04 us -> none  [the longest x1 1.12 us: on_device(): wanted = lax.dynamic_slice_in_dim(snapshots, away * 1664, 2432, 0)]
    pallas_call x4 -> x5, Pallas kernels: 39.6 us -> 36.7 us  [the longest x1 15.2 us: on_device(): call(last_merges_kernel, pltpu.VMEM((128, 512), BF16), name='last_merges')]
  transfers between devices with their start and end apart: 3 -> 3, of which waited for: 2 -> 2; matrix products, arithmetic and copies ran while one was open for 1% -> 0% of each run, Pallas kernels for 0% -> 0%
where the time goes in v1:
time: 182 us
  blocking collectives  126 us (69%)
  Pallas kernels  36.7 us (20%)
  starting transfers between devices  12 us (7%)
  waiting for transfers between devices  5.29 us (3%)
    all_to_all x8, blocking collectives, exchange(): return lax.all_to_all(parts, axis, split_axis=0, concat_axis=0, tiled=True)  126 us
    pallas_call x1, Pallas kernels, on_device(): call(last_merges_kernel, pltpu.VMEM((128, 512), BF16), name='last_merges')  15.2 us
    pallas_call x1, Pallas kernels, on_device(): call(leaf_and_merge_kernel, pltpu.VMEM((4, 528, 128), BF16), name='leaf_a...  13.4 us
    ppermute x1, starting transfers between devices, on_device(): other = lax.ppermute(wanted, 'core', [(0, 1), (1, 0)])  8.75 us
    pallas_call x1, Pallas kernels, on_device(): call(sections_kernel, (pltpu.VMEM((2048, 256), BF16), pltpu.VMEM((512, 12...  5.78 us
  transfers between devices with their start and end apart: 3, of which 2 were waited for; matrix products, arithmetic and copies ran while one was open for 0% of the time, Pallas kernels for 0%

profile of v1, /device:TPU:1, one launch (start us, length us, event | category | flops | bytes accessed | tf_op | source)
XLA Modules:
  0.0 181.6 jit_solution(13752999657544262947)
XLA Ops:
  0.0 2.0 %pack.1 = (bf16[2448,128]{1,0:T(8,128)(2,1)S(1)}, bf16[768,128]{1,0:T(8,128)(2,1)S(1)}, bf16[768,128]{1,0:T(8,128)(2,1)S(1)}) custom-call(s32[1]{0:T(128)} %bitcast.core_ref, f32[1,128]{1,0:T(1,128)} %bitcast.27, bf16[4096,128]{1,0:T(8,128)(2,1)} %snap.3, bf16[12288,128]{1,0:T(8,128)(2,1)} %bitcast.21), custom_call_target="tpu_custom_call" | custom-call | tf_op jit(solution)/shard_map/pack/pallas_call | solution.py:298
  2.0 8.7 %collective-permute-start = (bf16[2448,128]{1,0:T(8,128)(2,1)S(1)}, bf16[2448,128]{1,0:T(8,128)(2,1)S(1)}, u32[]{:S(2)}, u32[]{:S(2)}) collective-permute-start(bf16[2448,128]{1,0:T(8,128)(2,1)S(1)} %get-tuple-element.10), channel_id=1, source_target_pairs={{0,1},{1,0},{2,3},{3,2},{4,5},{5,4},{6,7},{7,6},{8,9},{9,8},{10,11... | collective-permute-start | bytes 1880072 | tf_op jit(solution)/shard_map/ppermute | solution.py:308
  10.7 1.3 collective-permute-start.1
  12.0 1.9 %collective-permute-start.2 = (bf16[768,128]{1,0:T(8,128)(2,1)S(1)}, bf16[768,128]{1,0:T(8,128)(2,1)S(1)}, u32[]{:S(2)}, u32[]{:S(2)}) collective-permute-start(bf16[768,128]{1,0:T(8,128)(2,1)S(1)} %get-tuple-element.12), channel_id=1, source_target_pairs={{1,8},{8,1},{9,16},{16,9},{17,24},{24,17},{25,32},{32,25},{33,40},... | collective-permute-start | bytes 589832 | tf_op jit(solution)/shard_map/ppermute | solution.py:307
  14.0 3.4 %collective-permute-done.1.halo_own = bf16[768,128]{1,0:T(8,128)(2,1)S(1)} collective-permute-done((bf16[768,128]{1,0:T(8,128)(2,1)S(1)}, bf16[768,128]{1,0:T(8,128)(2,1)S(1)}, u32[]{:S(2)}, u32[]{:S(2)}) %collective-permute-start.1) | collective-permute-done | bytes 196640 | tf_op jit(solution)/shard_map/ppermute | solution.py:306
  17.4 1.9 %collective-permute-done.2.halo_other = bf16[768,128]{1,0:T(8,128)(2,1)S(1)} collective-permute-done((bf16[768,128]{1,0:T(8,128)(2,1)S(1)}, bf16[768,128]{1,0:T(8,128)(2,1)S(1)}, u32[]{:S(2)}, u32[]{:S(2)}) %collective-permute-start.2) | collective-permute-done | bytes 196640 | tf_op jit(solution)/shard_map/ppermute | solution.py:307
  19.3 0.0 collective-permute-done.other
  19.3 5.8 %sections.1 = (bf16[2048,256]{1,0:T(8,128)(2,1)S(1)}, f32[512,128]{1,0:T(8,128)S(1)}) custom-call(s32[1]{0:T(128)} %bitcast.core_ref, f32[1,128]{1,0:T(1,128)} %bitcast.28, bf16[4096,128]{1,0:T(8,128)(2,1)} %snap.3, bf16[2448,128]{1,0:T(8,128)(2,1)S(1)} %collective-permute-done.other, bf16[768,128]{1,0:T(8,128)(2,1)S(1)} %collective-permute-done.1.halo_own, ...), custom_call_target="tpu_custom_call" | custom-call | tf_op jit(solution)/shard_map/sections/pallas_call | solution.py:309
  25.1 29.0 %all_to_all.40 = f32[128,4,128]{2,1,0:T(4,128)S(1)} all-to-all(f32[128,4,128]{2,1,0:T(4,128)S(1)} %bitcast.20), channel_id=1, replica_groups=mesh['mesh'=64,'x'=4,'core'=2] {'mesh','core'}, dimensions={0} | all-to-all | bytes 524288 | tf_op jit(solution)/shard_map/all_to_all | solution.py:19
  54.0 0.1 reduce_sum.27
  54.2 20.2 %all_to_all.41 = f32[128,4,128]{2,1,0:T(4,128)S(1)} all-to-all(f32[128,4,128]{2,1,0:T(4,128)S(1)} %broadcast_in_dim.17), channel_id=1, replica_groups=mesh['mesh'=64,'x'=4,'core'=2] {'mesh','core'}, dimensions={0} | all-to-all | bytes 524288 | tf_op jit(solution)/shard_map/all_to_all | solution.py:19
  74.5 13.4 %leaf_and_merge.1 = bf16[4,528,128]{2,1,0:T(8,128)(2,1)S(1)} custom-call(f32[512,128]{1,0:T(8,128)S(1)} %bitcast.18, bf16[256,128]{1,0:T(8,128)(2,1)} %sketch_ref.3, bf16[2048,256]{1,0:T(8,128)(2,1)S(1)} %get-tuple-element.14.state_ref), custom_call_target="tpu_custom_call" | custom-call | tf_op jit(solution)/shard_map/leaf_and_merge/pallas_call | solution.py:325
  87.8 12.9 %all_to_all.42.bases_ref = bf16[4,528,128]{2,1,0:T(8,128)(2,1)S(1)} all-to-all(bf16[4,528,128]{2,1,0:T(8,128)(2,1)S(1)} %leaf_and_merge.1), channel_id=1, replica_groups=mesh['mesh'=64,'x'=4,'core'=2] {'x'}, dimensions={0} | all-to-all | bytes 1081344 | tf_op jit(solution)/shard_map/all_to_all | solution.py:19
  100.7 0.4 cross.1
  101.1 11.9 %all_to_all.43 = f32[8,96,128]{2,1,0:T(8,128)S(1)} all-to-all(f32[8,96,128]{2,1,0:T(8,128)S(1)} %bitcast.17), channel_id=1, replica_groups=mesh['mesh'=64,'x'=4,'core'=2] {'x','core'}, dimensions={0} | all-to-all | bytes 786432 | tf_op jit(solution)/shard_map/all_to_all | solution.py:19
  113.1 14.9 %all_to_all.44 = f32[64,2,128]{2,1,0:T(2,128)S(1)} all-to-all(f32[64,2,128]{2,1,0:T(2,128)S(1)} %bitcast.25), channel_id=1, replica_groups=mesh['mesh'=64,'x'=4,'core'=2] {'mesh'}, dimensions={0} | all-to-all | bytes 131072 | tf_op jit(solution)/shard_map/all_to_all | solution.py:19
  128.0 0.1 reduce_sum.29
  128.1 15.1 %all_to_all.45 = f32[64,2,128]{2,1,0:T(2,128)S(1)} all-to-all(f32[64,2,128]{2,1,0:T(2,128)S(1)} %broadcast_in_dim.18), channel_id=1, replica_groups=mesh['mesh'=64,'x'=4,'core'=2] {'mesh'}, dimensions={0} | all-to-all | bytes 131072 | tf_op jit(solution)/shard_map/all_to_all | solution.py:19
  143.3 13.9 %all_to_all.46 = f32[8,96,128]{2,1,0:T(8,128)S(1)} all-to-all(f32[8,96,128]{2,1,0:T(8,128)S(1)} %broadcast_in_dim.19), channel_id=1, replica_groups=mesh['mesh'=64,'x'=4,'core'=2] {'x','core'}, dimensions={0} | all-to-all | bytes 786432 | tf_op jit(solution)/shard_map/all_to_all | solution.py:19
  157.2 15.2 %last_merges.1 = bf16[128,512]{1,0:T(8,128)(2,1)S(1)} custom-call(f32[768,128]{1,0:T(8,128)S(1)} %bitcast.16, bf16[256,128]{1,0:T(8,128)(2,1)} %sketch_ref.3, bf16[4,528,128]{2,1,0:T(8,128)(2,1)S(1)} %all_to_all.42.bases_ref), custom_call_target="tpu_custom_call" | custom-call | tf_op jit(solution)/shard_map/last_merges/pallas_call | solution.py:334
  172.3 8.5 %all_to_all.47 = bf16[8,16,512]{2,1,0:T(8,128)(2,1)S(1)} all-to-all(bf16[8,16,512]{2,1,0:T(8,128)(2,1)S(1)} %bitcast.19), channel_id=1, replica_groups=mesh['mesh'=64,'x'=4,'core'=2] {'x','core'}, dimensions={0} | all-to-all | bytes 262144 | tf_op jit(solution)/shard_map/all_to_all | solution.py:19
  180.8 0.1 copy.11
  180.9 0.7 reshape.37
  (6 shorter events, 0.1 us)
Async XLA Ops:
  2.0 17.3 %collective-permute-start = (bf16[2448,128]{1,0:T(8,128)(2,1)S(1)}, bf16[2448,128]{1,0:T(8,128)(2,1)S(1)}, u32[]{:S(2)}, u32[]{:S(2)}) collective-permute-start(bf16[2448,128]{1,0:T(8,128)(2,1)S(1)} %get-tuple-element.10), channel_id=1, source_target_pairs={{0,1},{1,0},{2,3},{3,2},{4,5},{5,4},{6,7},{7,6},{8,9},{9,8},{10,11... | collective-permute-start | bytes 1880072 | tf_op jit(solution)/shard_map/ppermute | solution.py:308
  10.7 6.6 %collective-permute-start.1 = (bf16[768,128]{1,0:T(8,128)(2,1)S(1)}, bf16[768,128]{1,0:T(8,128)(2,1)S(1)}, u32[]{:S(2)}, u32[]{:S(2)}) collective-permute-start(bf16[768,128]{1,0:T(8,128)(2,1)S(1)} %get-tuple-element.11), channel_id=1, source_target_pairs={{0,8},{9,1},{8,16},{17,9},{16,24},{25,17},{24,32},{33,25},{32,40},... | collective-permute-start | bytes 589832 | tf_op jit(solution)/shard_map/ppermute | solution.py:306
  12.0 7.2 %collective-permute-start.2 = (bf16[768,128]{1,0:T(8,128)(2,1)S(1)}, bf16[768,128]{1,0:T(8,128)(2,1)S(1)}, u32[]{:S(2)}, u32[]{:S(2)}) collective-permute-start(bf16[768,128]{1,0:T(8,128)(2,1)S(1)} %get-tuple-element.12), channel_id=1, source_target_pairs={{1,8},{8,1},{9,16},{16,9},{17,24},{24,17},{25,32},{32,25},{33,40},... | collective-permute-start | bytes 589832 | tf_op jit(solution)/shard_map/ppermute | solution.py:307

commit v2 on v1

--- a/solution.py
+++ b/solution.py
@@ -47,59 +47,81 @@
     )
 
 
-def stacked_rows(rows):
+def stacked_rows(rows, count):
     sublane = lax.broadcasted_iota(jnp.int32, rows[0].shape, 0)
-    eights = []
+    stacks = [[] for _ in range(count)]
     for first in range(0, len(rows), 8):
-        eight = rows[first]
-        for i in range(1, 8):
-            eight = jnp.where(sublane == i, rows[first + i], eight)
-        eights.append(eight)
-    return jnp.concatenate(eights, 0)
+        if count == 1:
+            eight = rows[first]
+            for i in range(1, 8):
+                eight = jnp.where(sublane == i, rows[first + i], eight)
+            stacks[0].append(eight)
+            continue
+        fours = []
+        for begin in (first, first + 4):
+            four = rows[begin]
+            for i in range(1, 4):
+                four = jnp.where(sublane % 4 == i, rows[begin + i], four)
+            fours.append(four)
+        upper = sublane < 4
+        stacks[0].append(jnp.where(upper, fours[0], pltpu.roll(fours[1], 4, 0)))
+        stacks[1].append(jnp.where(upper, pltpu.roll(fours[0], 4, 0), fours[1]))
+    return [jnp.concatenate(stack, 0) for stack in stacks]
 
 
 def eliminate(grams):
+    count = len(grams)
     size = grams[0].shape[0]
     shape = (8, size)
-    lane = lax.broadcasted_iota(jnp.int32, (1, size), 1)
+    upper = lax.broadcasted_iota(jnp.int32, shape, 0) < 4
+    lane = lax.broadcasted_iota(jnp.int32, shape, 1)
     row_of = lax.broadcasted_iota(jnp.int32, (size, size), 0)
     column_of = lax.broadcasted_iota(jnp.int32, (size, size), 1)
     unit = jnp.where(row_of == column_of, 1.0, 0.0).astype(F32)
+
+    def spread(parts):
+        wide = [jnp.broadcast_to(part, shape) for part in parts]
+        return wide[0] if count == 1 else jnp.where(upper, *wide)
+
     work = [(gram, unit) for gram in grams]
     done = [[] for _ in grams]
-    scales = [jnp.zeros((1, size), F32) for _ in grams]
+    scales = jnp.zeros(shape, F32)
     for start in range(0, size, PANEL):
-        following = []
-        for index, (gram, inverse) in enumerate(work):
-            value = {
-                (i, j): jnp.broadcast_to(gram[i : i + 1, start + j : start + j + 1], shape)
-                for i in range(PANEL)
-                for j in range(i, PANEL)
-            }
-            rows = [jnp.broadcast_to(gram[i : i + 1], shape) for i in range(PANEL)]
-            rows_inverse = [jnp.broadcast_to(inverse[i : i + 1], shape) for i in range(PANEL)]
-            ratio = []
-            for i in range(PANEL):
-                inverse_pivot = 1.0 / value[i, i]
-                ratio.append(inverse_pivot)
-                scales[index] = jnp.where(lane == start + i, value[i, i][:1], scales[index])
-                for j in range(i + 1, PANEL):
-                    step = value[i, j] * inverse_pivot
-                    for k in range(j, PANEL):
-                        value[j, k] = value[j, k] - step * value[i, k]
-                    rows[j] = rows[j] - step * rows[i]
-                    rows_inverse[j] = rows_inverse[j] - step * rows_inverse[i]
-            finished = stacked_rows(rows_inverse)
-            done[index].append(finished)
-            if start + PANEL < size:
-                scaled = stacked_rows([row * by for row, by in zip(rows, ratio)])
-                both = jnp.concatenate([stacked_rows(rows), finished], 1)
-                update = precise(scaled, both, ((0,), (0,)))[start + PANEL :]
+        rows = [spread([gram[i : i + 1] for gram, _ in work]) for i in range(PANEL)]
+        value = {
+            (i, j): jnp.broadcast_to(rows[i][:, start + j : start + j + 1], shape)
+            for i in range(PANEL)
+            for j in range(i, PANEL)
+        }
+        rows_inverse = [spread([inverse[i : i + 1] for _, inverse in work]) for i in range(PANEL)]
+        ratio = []
+        for i in range(PANEL):
+            inverse_pivot = 1.0 / value[i, i]
+            ratio.append(inverse_pivot)
+            scales = jnp.where(lane == start + i, value[i, i], scales)
+            for j in range(i + 1, PANEL):
+                step = value[i, j] * inverse_pivot
+                for k in range(j, PANEL):
+                    value[j, k] = value[j, k] - step * value[i, k]
+                rows[j] = rows[j] - step * rows[i]
+                rows_inverse[j] = rows_inverse[j] - step * rows_inverse[i]
+        finished = stacked_rows(rows_inverse, count)
+        for parts, part in zip(done, finished):
+            parts.append(part)
+        if start + PANEL < size:
+            scaled = stacked_rows([row * by for row, by in zip(rows, ratio)], count)
+            reduced = stacked_rows(rows, count)
+            following = []
+            for index, (gram, inverse) in enumerate(work):
+                both = jnp.concatenate([reduced[index], finished[index]], 1)
+                update = precise(scaled[index], both, ((0,), (0,)))[start + PANEL :]
                 following.append(
                     (gram[PANEL:] - update[:, :size], inverse[PANEL:] - update[:, size:])
                 )
-        work = following
-    return [jnp.concatenate(parts, 0) for parts in done], scales
+            work = following
+    return [jnp.concatenate(parts, 0) for parts in done], [
+        scales[4 * index : 4 * index + 1] for index in range(count)
+    ]
 
 
 def pack_kernel(core_ref, rate_ref, snap, coupling, wanted, edge_own, edge_other, sems):
@@ -210,34 +232,33 @@
         [precise(lower, sketch[:128], ((0,), (0,))), precise(upper, sketch[128:], ((0,), (0,)))], 0
     )
     merged_gram = precise(mixing, precise(gram, mixing, ((1,), (0,))), ((0,), (0,)))
-    (merged,), (scale,) = eliminate([merged_gram])
+    (merged,), _ = eliminate([merged_gram])
     factor = jnp.concatenate(terms_of(precise(mixing, merged, ((1,), (1,)), 2), 2), 1)
-    tail = jnp.concatenate([*terms_of(scale, 3), jnp.zeros((13, 128), BF16)], 0)
     for part in range(4):
         pieces = dot(state_ref[part * 512 : part * 512 + 512], factor, ((1,), (0,)))
-        basis_ref[part, :512] = (pieces[:, :128] + pieces[:, 128:]).astype(BF16)
-        basis_ref[part, 512:] = tail
-
-
-PAIRS = ((0, 1), (2, 3), (0, 2), (0, 3), (1, 2), (1, 3))
-
-
-def cross_kernel(bases_ref, cross_ref):
-    for at, (i, j) in enumerate(PAIRS):
-        cross_ref[at * 128 : at * 128 + 128] = dot(
-            bases_ref[i, :512], bases_ref[j, :512], ((0,), (0,))
-        )
-
-
-def last_merges_kernel(cross_ref, sketch_ref, bases_ref, out_ref):
+        basis_ref[part] = (pieces[:, :128] + pieces[:, 128:]).astype(BF16)
+
+
+def merge_grams_kernel(bases_ref, sketch_ref, gram_ref):
+    sketch = sketch_ref[...]
+    low = jnp.concatenate([bases_ref[0], bases_ref[1]], 1)
+    high = jnp.concatenate([bases_ref[2], bases_ref[3]], 1)
+    grams = jnp.concatenate(
+        [dot(low, low, ((0,), (0,))), dot(high, high, ((0,), (0,))), dot(low, high, ((0,), (0,)))], 0
+    )
+    mixed = precise(grams, sketch, ((1,), (0,)))
+    mixed = precise(
+        sketch, jnp.concatenate([mixed[:256], mixed[256:512], mixed[512:]], 1), ((0,), (0,))
+    )
+    for at in range(3):
+        gram_ref[at * 128 : at * 128 + 128] = mixed[:, at * 128 : at * 128 + 128]
+    gram_ref[384:] = jnp.zeros((128, 128), F32)
+
+
+def last_merges_kernel(gram_ref, sketch_ref, bases_ref, out_ref):
     sketch = sketch_ref[...]
     row_of = lax.broadcasted_iota(jnp.int32, (128, 128), 0)
     column_of = lax.broadcasted_iota(jnp.int32, (128, 128), 1)
-    cross = [cross_ref[at * 128 : at * 128 + 128] for at in range(6)]
-    scales = []
-    for i in range(4):
-        tail = bases_ref[i, 512:].astype(F32)
-        scales.append(tail[0:1] + tail[1:2] + tail[2:3])
 
     def diagonal(scale):
         return jnp.where(row_of == column_of, jnp.broadcast_to(scale, (128, 128)), 0.0)
@@ -252,13 +273,8 @@
         )
         return precise(sketch, precise(gram, sketch, ((1,), (0,))), ((0,), (0,)))
 
-    between = jnp.concatenate(
-        [jnp.concatenate([cross[2], cross[3]], 1), jnp.concatenate([cross[4], cross[5]], 1)], 0
-    )
-    between = precise(sketch, precise(between, sketch, ((1,), (0,))), ((0,), (0,)))
-    pair_grams = [joined(scales[0], scales[1], cross[0]), joined(scales[2], scales[3], cross[1])]
-    (low, high), (low_scale, high_scale) = eliminate(pair_grams)
-    between = precise(low, precise(between, high, ((1,), (1,))), ((1,), (0,)))
+    (low, high), (low_scale, high_scale) = eliminate([gram_ref[:128], gram_ref[128:256]])
+    between = precise(low, precise(gram_ref[256:384], high, ((1,), (1,))), ((1,), (0,)))
     root_gram = joined(low_scale, high_scale, between)
     weights = jnp.concatenate(
         [
@@ -269,7 +285,7 @@
     )
     (root,), _ = eliminate([root_gram])
     weights = jnp.concatenate(terms_of(precise(weights, root, ((1,), (1,)), 2), 2), 1)
-    pieces = dot(jnp.concatenate([bases_ref[i, :512] for i in range(4)], 1), weights, ((1,), (0,)))
+    pieces = dot(jnp.concatenate([bases_ref[i] for i in range(4)], 1), weights, ((1,), (0,)))
     out_ref[...] = (pieces[:, :128] + pieces[:, 128:]).T.astype(BF16)
 
 
@@ -323,17 +339,16 @@
     own = exchange(gram.reshape(128, 4, 128), GROUP).sum(0)
     gram = copies_to(own, GROUP).reshape(512, 128)
     bases = call(
-        leaf_and_merge_kernel, pltpu.VMEM((4, 528, 128), BF16), name="leaf_and_merge"
+        leaf_and_merge_kernel, pltpu.VMEM((4, 512, 128), BF16), name="leaf_and_merge"
     )(on_chip(gram), sketch, on_chip(state))
     bases = on_chip(exchange(bases, "x"))
-    cross = call(cross_kernel, pltpu.VMEM((768, 128), F32), name="cross")(bases)
-    own = exchange(cross.reshape(8, 96, 128), PARAM).sum(0)
-    own = jnp.pad(own, ((0, 32), (0, 0)))
-    own = copies_to(exchange(own.reshape(64, 2, 128), "mesh").sum(0), "mesh")
-    cross = copies_to(own.reshape(128, 128)[:96], PARAM).reshape(768, 128)
+    gram = call(merge_grams_kernel, pltpu.VMEM((512, 128), F32), name="merge_grams")(bases, sketch)
+    own = exchange(gram.reshape(128, 4, 128), GROUP).sum(0)
+    own = copies_to(own, "x").sum(0)
+    gram = copies_to(own, GROUP).reshape(512, 128)
     turned = call(
         last_merges_kernel, pltpu.VMEM((128, 512), BF16), name="last_merges"
-    )(on_chip(cross), sketch, bases)
+    )(on_chip(gram), sketch, bases)
     turned = exchange(turned.reshape(8, 16, 512), PARAM)
     return turned.reshape(4, 2, 16, 512).transpose(1, 0, 3, 2).reshape(4096, 16)
 

time: 182 us -> 172 us (0.945)
  blocking collectives: 126 us -> 119 us
  Pallas kernels: 36.7 us -> 33.1 us
    all_to_all x8 -> x7, blocking collectives: 126 us -> 119 us  [exchange(): return lax.all_to_all(parts, axis, split_axis=0, concat_axis=0, tiled=True)]
    pallas_call x1, Pallas kernels: 15.2 us -> 11.7 us  [on_device(): call(last_merges_kernel, pltpu.VMEM((128, 512), BF16), name='last_merges')]
where the time goes in v2:
time: 172 us; the launch traced here: 171 us
  blocking collectives  119 us (69%)
  Pallas kernels  33.1 us (19%)
  starting transfers between devices  12 us (7%)
  waiting for transfers between devices  5.29 us (3%)
    all_to_all x7, blocking collectives, exchange(): return lax.all_to_all(parts, axis, split_axis=0, concat_axis=0, tiled=True)  119 us
    pallas_call x1, Pallas kernels, on_device(): call(last_merges_kernel, pltpu.VMEM((128, 512), BF16), name='last_merges')  11.7 us
    pallas_call x1, Pallas kernels, on_device(): call(leaf_and_merge_kernel, pltpu.VMEM((4, 512, 128), BF16), name='leaf_a...  11.6 us
    ppermute x1, starting transfers between devices, on_device(): other = lax.ppermute(wanted, 'core', [(0, 1), (1, 0)])  8.75 us
    pallas_call x1, Pallas kernels, on_device(): call(sections_kernel, (pltpu.VMEM((2048, 256), BF16), pltpu.VMEM((512, 12...  5.78 us
  transfers between devices with their start and end apart: 3, of which 2 were waited for; matrix products, arithmetic and copies ran while one was open for 0% of the time, Pallas kernels for 0%

profile of v2, /device:TPU:1, one launch (start us, length us, event | category | flops | bytes accessed | tf_op | source)
XLA Modules:
  0.0 171.1 jit_solution(15881731882286711818)
XLA Ops:
  0.0 2.0 %pack.1 = (bf16[2448,128]{1,0:T(8,128)(2,1)S(1)}, bf16[768,128]{1,0:T(8,128)(2,1)S(1)}, bf16[768,128]{1,0:T(8,128)(2,1)S(1)}) custom-call(s32[1]{0:T(128)} %bitcast.core_ref, f32[1,128]{1,0:T(1,128)} %bitcast.23, bf16[4096,128]{1,0:T(8,128)(2,1)} %snap.3, bf16[12288,128]{1,0:T(8,128)(2,1)} %bitcast.19), custom_call_target="tpu_custom_call" | custom-call | tf_op jit(solution)/shard_map/pack/pallas_call | solution.py:314
  2.0 8.7 %collective-permute-start = (bf16[2448,128]{1,0:T(8,128)(2,1)S(1)}, bf16[2448,128]{1,0:T(8,128)(2,1)S(1)}, u32[]{:S(2)}, u32[]{:S(2)}) collective-permute-start(bf16[2448,128]{1,0:T(8,128)(2,1)S(1)} %get-tuple-element.10), channel_id=1, source_target_pairs={{0,1},{1,0},{2,3},{3,2},{4,5},{5,4},{6,7},{7,6},{8,9},{9,8},{10,11... | collective-permute-start | bytes 1880072 | tf_op jit(solution)/shard_map/ppermute | solution.py:324
  10.7 1.3 collective-permute-start.1
  12.0 1.9 %collective-permute-start.2 = (bf16[768,128]{1,0:T(8,128)(2,1)S(1)}, bf16[768,128]{1,0:T(8,128)(2,1)S(1)}, u32[]{:S(2)}, u32[]{:S(2)}) collective-permute-start(bf16[768,128]{1,0:T(8,128)(2,1)S(1)} %get-tuple-element.12), channel_id=1, source_target_pairs={{1,8},{8,1},{9,16},{16,9},{17,24},{24,17},{25,32},{32,25},{33,40},... | collective-permute-start | bytes 589832 | tf_op jit(solution)/shard_map/ppermute | solution.py:323
  14.0 3.4 %collective-permute-done.1.halo_own = bf16[768,128]{1,0:T(8,128)(2,1)S(1)} collective-permute-done((bf16[768,128]{1,0:T(8,128)(2,1)S(1)}, bf16[768,128]{1,0:T(8,128)(2,1)S(1)}, u32[]{:S(2)}, u32[]{:S(2)}) %collective-permute-start.1) | collective-permute-done | bytes 196640 | tf_op jit(solution)/shard_map/ppermute | solution.py:322
  17.4 1.9 %collective-permute-done.2.halo_other = bf16[768,128]{1,0:T(8,128)(2,1)S(1)} collective-permute-done((bf16[768,128]{1,0:T(8,128)(2,1)S(1)}, bf16[768,128]{1,0:T(8,128)(2,1)S(1)}, u32[]{:S(2)}, u32[]{:S(2)}) %collective-permute-start.2) | collective-permute-done | bytes 196640 | tf_op jit(solution)/shard_map/ppermute | solution.py:323
  19.3 0.0 collective-permute-done.other
  19.3 5.8 %sections.1 = (bf16[2048,256]{1,0:T(8,128)(2,1)S(1)}, f32[512,128]{1,0:T(8,128)S(1)}) custom-call(s32[1]{0:T(128)} %bitcast.core_ref, f32[1,128]{1,0:T(1,128)} %bitcast.24, bf16[4096,128]{1,0:T(8,128)(2,1)} %snap.3, bf16[2448,128]{1,0:T(8,128)(2,1)S(1)} %collective-permute-done.other, bf16[768,128]{1,0:T(8,128)(2,1)S(1)} %collective-permute-done.1.halo_own, ...), custom_call_target="tpu_custom_call" | custom-call | tf_op jit(solution)/shard_map/sections/pallas_call | solution.py:325
  25.1 29.0 %all_to_all.35 = f32[128,4,128]{2,1,0:T(4,128)S(1)} all-to-all(f32[128,4,128]{2,1,0:T(4,128)S(1)} %bitcast.18), channel_id=1, replica_groups=mesh['mesh'=64,'x'=4,'core'=2] {'mesh','core'}, dimensions={0} | all-to-all | bytes 524288 | tf_op jit(solution)/shard_map/all_to_all | solution.py:19
  54.0 0.1 reduce_sum.27
  54.2 20.2 %all_to_all.36 = f32[128,4,128]{2,1,0:T(4,128)S(1)} all-to-all(f32[128,4,128]{2,1,0:T(4,128)S(1)} %broadcast_in_dim.17), channel_id=1, replica_groups=mesh['mesh'=64,'x'=4,'core'=2] {'mesh','core'}, dimensions={0} | all-to-all | bytes 524288 | tf_op jit(solution)/shard_map/all_to_all | solution.py:19
  74.5 11.6 %leaf_and_merge.1 = bf16[4,512,128]{2,1,0:T(8,128)(2,1)S(1)} custom-call(f32[512,128]{1,0:T(8,128)S(1)} %bitcast.16, bf16[256,128]{1,0:T(8,128)(2,1)} %sketch_ref.5, bf16[2048,256]{1,0:T(8,128)(2,1)S(1)} %get-tuple-element.14.state_ref), custom_call_target="tpu_custom_call" | custom-call | tf_op jit(solution)/shard_map/leaf_and_merge/pallas_call | solution.py:341
  86.0 12.4 %all_to_all.37.bases_ref = bf16[4,512,128]{2,1,0:T(8,128)(2,1)S(1)} all-to-all(bf16[4,512,128]{2,1,0:T(8,128)(2,1)S(1)} %leaf_and_merge.1), channel_id=1, replica_groups=mesh['mesh'=64,'x'=4,'core'=2] {'x'}, dimensions={0} | all-to-all | bytes 1048576 | tf_op jit(solution)/shard_map/all_to_all | solution.py:19
  98.5 2.1 %merge_grams.1 = f32[512,128]{1,0:T(8,128)S(1)} custom-call(bf16[4,512,128]{2,1,0:T(8,128)(2,1)S(1)} %all_to_all.37.bases_ref, bf16[256,128]{1,0:T(8,128)(2,1)} %sketch_ref.5), custom_call_target="tpu_custom_call" | custom-call | tf_op jit(solution)/shard_map/merge_grams/pallas_call | solution.py:345
  100.6 21.7 %all_to_all.38 = f32[128,4,128]{2,1,0:T(4,128)S(1)} all-to-all(f32[128,4,128]{2,1,0:T(4,128)S(1)} %bitcast.14), channel_id=1, replica_groups=mesh['mesh'=64,'x'=4,'core'=2] {'mesh','core'}, dimensions={0} | all-to-all | bytes 524288 | tf_op jit(solution)/shard_map/all_to_all | solution.py:19
  122.2 0.1 reduce_sum.28
  122.4 6.5 %all_to_all.39 = f32[4,4,128]{2,1,0:T(4,128)S(1)} all-to-all(f32[4,4,128]{2,1,0:T(4,128)S(1)} %broadcast_in_dim.18), channel_id=1, replica_groups=mesh['mesh'=64,'x'=4,'core'=2] {'x'}, dimensions={0} | all-to-all | bytes 16384 | tf_op jit(solution)/shard_map/all_to_all | solution.py:19
  128.9 21.6 %all_to_all.40 = f32[128,4,128]{2,1,0:T(4,128)S(1)} all-to-all(f32[128,4,128]{2,1,0:T(4,128)S(1)} %broadcast_in_dim.19), channel_id=1, replica_groups=mesh['mesh'=64,'x'=4,'core'=2] {'mesh','core'}, dimensions={0} | all-to-all | bytes 524288 | tf_op jit(solution)/shard_map/all_to_all | solution.py:19
  150.5 11.7 %last_merges.1 = bf16[128,512]{1,0:T(8,128)(2,1)S(1)} custom-call(f32[512,128]{1,0:T(8,128)S(1)} %bitcast.15, bf16[256,128]{1,0:T(8,128)(2,1)} %sketch_ref.5, bf16[4,512,128]{2,1,0:T(8,128)(2,1)S(1)} %all_to_all.37.bases_ref), custom_call_target="tpu_custom_call" | custom-call | tf_op jit(solution)/shard_map/last_merges/pallas_call | solution.py:349
  162.2 8.0 %all_to_all.41 = bf16[8,16,512]{2,1,0:T(8,128)(2,1)S(1)} all-to-all(bf16[8,16,512]{2,1,0:T(8,128)(2,1)S(1)} %bitcast.17), channel_id=1, replica_groups=mesh['mesh'=64,'x'=4,'core'=2] {'x','core'}, dimensions={0} | all-to-all | bytes 262144 | tf_op jit(solution)/shard_map/all_to_all | solution.py:19
  170.2 0.1 copy.8
  170.3 0.7 reshape.31
  (4 shorter events, 0.1 us)
Async XLA Ops:
  2.0 17.3 %collective-permute-start = (bf16[2448,128]{1,0:T(8,128)(2,1)S(1)}, bf16[2448,128]{1,0:T(8,128)(2,1)S(1)}, u32[]{:S(2)}, u32[]{:S(2)}) collective-permute-start(bf16[2448,128]{1,0:T(8,128)(2,1)S(1)} %get-tuple-element.10), channel_id=1, source_target_pairs={{0,1},{1,0},{2,3},{3,2},{4,5},{5,4},{6,7},{7,6},{8,9},{9,8},{10,11... | collective-permute-start | bytes 1880072 | tf_op jit(solution)/shard_map/ppermute | solution.py:324
  10.7 6.6 %collective-permute-start.1 = (bf16[768,128]{1,0:T(8,128)(2,1)S(1)}, bf16[768,128]{1,0:T(8,128)(2,1)S(1)}, u32[]{:S(2)}, u32[]{:S(2)}) collective-permute-start(bf16[768,128]{1,0:T(8,128)(2,1)S(1)} %get-tuple-element.11), channel_id=1, source_target_pairs={{0,8},{9,1},{8,16},{17,9},{16,24},{25,17},{24,32},{33,25},{32,40},... | collective-permute-start | bytes 589832 | tf_op jit(solution)/shard_map/ppermute | solution.py:322
  12.0 7.2 %collective-permute-start.2 = (bf16[768,128]{1,0:T(8,128)(2,1)S(1)}, bf16[768,128]{1,0:T(8,128)(2,1)S(1)}, u32[]{:S(2)}, u32[]{:S(2)}) collective-permute-start(bf16[768,128]{1,0:T(8,128)(2,1)S(1)} %get-tuple-element.12), channel_id=1, source_target_pairs={{1,8},{8,1},{9,16},{16,9},{17,24},{24,17},{25,32},{32,25},{33,40},... | collective-permute-start | bytes 589832 | tf_op jit(solution)/shard_map/ppermute | solution.py:323

commit v3 on v2

--- a/solution.py
+++ b/solution.py
@@ -221,11 +221,14 @@
         piece = state_out[part * 512 : part * 512 + 512]
         gram = gram + dot(piece, piece, ((0,), (0,)))
     gram_out[:256] = gram[:, :128]
-    gram_out[256:] = gram[:, 128:]
+    gram_out[256:] = gram[128:, 128:]
 
 
 def leaf_and_merge_kernel(gram_ref, sketch_ref, state_ref, basis_ref):
-    gram = jnp.concatenate([gram_ref[:256], gram_ref[256:]], 1)
+    across = gram_ref[128:256]
+    gram = jnp.concatenate(
+        [gram_ref[:256], jnp.concatenate([across.T, gram_ref[256:]], 0)], 1
+    )
     sketch = sketch_ref[...]
     (lower, upper), _ = eliminate([gram[:128, :128], gram[128:, 128:]])
     mixing = jnp.concatenate(
@@ -252,7 +255,6 @@
     )
     for at in range(3):
         gram_ref[at * 128 : at * 128 + 128] = mixed[:, at * 128 : at * 128 + 128]
-    gram_ref[384:] = jnp.zeros((128, 128), F32)
 
 
 def last_merges_kernel(gram_ref, sketch_ref, bases_ref, out_ref):
@@ -324,7 +326,7 @@
     other = lax.ppermute(wanted, "core", [(0, 1), (1, 0)])
     state, gram = call(
         sections_kernel,
-        (pltpu.VMEM((2048, 256), BF16), pltpu.VMEM((512, 128), F32)),
+        (pltpu.VMEM((2048, 256), BF16), pltpu.VMEM((384, 128), F32)),
         in_specs=[smem, vmem, hbm, vmem, vmem, vmem, hbm],
         out_specs=(vmem, vmem),
         scratch_shapes=[
@@ -336,16 +338,16 @@
         name="sections",
     )(place, rate, snapshots, on_chip(other), on_chip(halo_own), on_chip(halo_other), operators)
 
-    own = exchange(gram.reshape(128, 4, 128), GROUP).sum(0)
-    gram = copies_to(own, GROUP).reshape(512, 128)
+    own = exchange(gram.reshape(128, 1, 384), GROUP).sum(0)
+    gram = copies_to(own, GROUP).reshape(384, 128)
     bases = call(
         leaf_and_merge_kernel, pltpu.VMEM((4, 512, 128), BF16), name="leaf_and_merge"
     )(on_chip(gram), sketch, on_chip(state))
     bases = on_chip(exchange(bases, "x"))
-    gram = call(merge_grams_kernel, pltpu.VMEM((512, 128), F32), name="merge_grams")(bases, sketch)
-    own = exchange(gram.reshape(128, 4, 128), GROUP).sum(0)
+    gram = call(merge_grams_kernel, pltpu.VMEM((384, 128), F32), name="merge_grams")(bases, sketch)
+    own = exchange(gram.reshape(128, 1, 384), GROUP).sum(0)
     own = copies_to(own, "x").sum(0)
-    gram = copies_to(own, GROUP).reshape(512, 128)
+    gram = copies_to(own, GROUP).reshape(384, 128)
     turned = call(
         last_merges_kernel, pltpu.VMEM((128, 512), BF16), name="last_merges"
     )(on_chip(gram), sketch, bases)

time: 172 us -> 167 us (0.971)
  blocking collectives: 119 us -> 114 us
    all_to_all x7, blocking collectives: 119 us -> 114 us  [exchange(): return lax.all_to_all(parts, axis, split_axis=0, concat_axis=0, tiled=True)]
where the time goes in v3:
time: 167 us; the launch traced here: 166 us
  blocking collectives  114 us (68%)
  Pallas kernels  33.1 us (20%)
  starting transfers between devices  12 us (7%)
  waiting for transfers between devices  5.29 us (3%)
    all_to_all x7, blocking collectives, exchange(): return lax.all_to_all(parts, axis, split_axis=0, concat_axis=0, tiled=True)  114 us
    pallas_call x1, Pallas kernels, on_device(): call(last_merges_kernel, pltpu.VMEM((128, 512), BF16), name='last_merges')  11.7 us
    pallas_call x1, Pallas kernels, on_device(): call(leaf_and_merge_kernel, pltpu.VMEM((4, 512, 128), BF16), name='leaf_a...  11.6 us
    ppermute x1, starting transfers between devices, on_device(): other = lax.ppermute(wanted, 'core', [(0, 1), (1, 0)])  8.75 us
    pallas_call x1, Pallas kernels, on_device(): call(sections_kernel, (pltpu.VMEM((2048, 256), BF16), pltpu.VMEM((384, 12...  5.78 us
    ppermute x1, waiting for transfers between devices, on_device(): halo_own = lax.ppermute(edge_own, GROUP, same)  3.42 us
  transfers between devices with their start and end apart: 3, of which 2 were waited for; matrix products, arithmetic and copies ran while one was open for 0% of the time, Pallas kernels for 0%

profile of v3, /device:TPU:1, one launch (start us, length us, event | category | flops | bytes accessed | tf_op | source)
XLA Modules:
  0.0 166.2 jit_solution(3521110118836425183)
XLA Ops:
  0.0 2.0 %pack.1 = (bf16[2448,128]{1,0:T(8,128)(2,1)S(1)}, bf16[768,128]{1,0:T(8,128)(2,1)S(1)}, bf16[768,128]{1,0:T(8,128)(2,1)S(1)}) custom-call(s32[1]{0:T(128)} %bitcast.core_ref, f32[1,128]{1,0:T(1,128)} %bitcast.23, bf16[4096,128]{1,0:T(8,128)(2,1)} %snap.3, bf16[12288,128]{1,0:T(8,128)(2,1)} %bitcast.19), custom_call_target="tpu_custom_call" | custom-call | tf_op jit(solution)/shard_map/pack/pallas_call | solution.py:316
  2.0 8.7 %collective-permute-start = (bf16[2448,128]{1,0:T(8,128)(2,1)S(1)}, bf16[2448,128]{1,0:T(8,128)(2,1)S(1)}, u32[]{:S(2)}, u32[]{:S(2)}) collective-permute-start(bf16[2448,128]{1,0:T(8,128)(2,1)S(1)} %get-tuple-element.10), channel_id=1, source_target_pairs={{0,1},{1,0},{2,3},{3,2},{4,5},{5,4},{6,7},{7,6},{8,9},{9,8},{10,11... | collective-permute-start | bytes 1880072 | tf_op jit(solution)/shard_map/ppermute | solution.py:326
  10.7 1.3 collective-permute-start.1
  12.0 1.9 %collective-permute-start.2 = (bf16[768,128]{1,0:T(8,128)(2,1)S(1)}, bf16[768,128]{1,0:T(8,128)(2,1)S(1)}, u32[]{:S(2)}, u32[]{:S(2)}) collective-permute-start(bf16[768,128]{1,0:T(8,128)(2,1)S(1)} %get-tuple-element.12), channel_id=1, source_target_pairs={{1,8},{8,1},{9,16},{16,9},{17,24},{24,17},{25,32},{32,25},{33,40},... | collective-permute-start | bytes 589832 | tf_op jit(solution)/shard_map/ppermute | solution.py:325
  14.0 3.4 %collective-permute-done.1.halo_own = bf16[768,128]{1,0:T(8,128)(2,1)S(1)} collective-permute-done((bf16[768,128]{1,0:T(8,128)(2,1)S(1)}, bf16[768,128]{1,0:T(8,128)(2,1)S(1)}, u32[]{:S(2)}, u32[]{:S(2)}) %collective-permute-start.1) | collective-permute-done | bytes 196640 | tf_op jit(solution)/shard_map/ppermute | solution.py:324
  17.4 1.9 %collective-permute-done.2.halo_other = bf16[768,128]{1,0:T(8,128)(2,1)S(1)} collective-permute-done((bf16[768,128]{1,0:T(8,128)(2,1)S(1)}, bf16[768,128]{1,0:T(8,128)(2,1)S(1)}, u32[]{:S(2)}, u32[]{:S(2)}) %collective-permute-start.2) | collective-permute-done | bytes 196640 | tf_op jit(solution)/shard_map/ppermute | solution.py:325
  19.3 0.0 collective-permute-done.other
  19.3 5.8 %sections.1 = (bf16[2048,256]{1,0:T(8,128)(2,1)S(1)}, f32[384,128]{1,0:T(8,128)S(1)}) custom-call(s32[1]{0:T(128)} %bitcast.core_ref, f32[1,128]{1,0:T(1,128)} %bitcast.24, bf16[4096,128]{1,0:T(8,128)(2,1)} %snap.3, bf16[2448,128]{1,0:T(8,128)(2,1)S(1)} %collective-permute-done.other, bf16[768,128]{1,0:T(8,128)(2,1)S(1)} %collective-permute-done.1.halo_own, ...), custom_call_target="tpu_custom_call" | custom-call | tf_op jit(solution)/shard_map/sections/pallas_call | solution.py:327
  25.1 27.7 %all_to_all.35 = f32[128,1,384]{2,1,0:T(1,128)S(1)} all-to-all(f32[128,1,384]{2,1,0:T(1,128)S(1)} %bitcast.18), channel_id=1, replica_groups=mesh['mesh'=64,'x'=4,'core'=2] {'mesh','core'}, dimensions={0} | all-to-all | bytes 393216 | tf_op jit(solution)/shard_map/all_to_all | solution.py:19
  52.8 0.2 reduce_sum.27
  52.9 0.1 broadcast_in_dim.17
  53.0 19.0 %all_to_all.36 = f32[128,1,384]{2,1,0:T(1,128)S(1)} all-to-all(f32[128,1,384]{2,1,0:T(1,128)S(1)} %broadcast_in_dim.17), channel_id=1, replica_groups=mesh['mesh'=64,'x'=4,'core'=2] {'mesh','core'}, dimensions={0} | all-to-all | bytes 393216 | tf_op jit(solution)/shard_map/all_to_all | solution.py:19
  72.0 11.6 %leaf_and_merge.1 = bf16[4,512,128]{2,1,0:T(8,128)(2,1)S(1)} custom-call(f32[384,128]{1,0:T(8,128)S(1)} %bitcast.14, bf16[256,128]{1,0:T(8,128)(2,1)} %sketch_ref.5, bf16[2048,256]{1,0:T(8,128)(2,1)S(1)} %get-tuple-element.14.state_ref), custom_call_target="tpu_custom_call" | custom-call | tf_op jit(solution)/shard_map/leaf_and_merge/pallas_call | solution.py:343
  83.6 12.4 %all_to_all.37.bases_ref = bf16[4,512,128]{2,1,0:T(8,128)(2,1)S(1)} all-to-all(bf16[4,512,128]{2,1,0:T(8,128)(2,1)S(1)} %leaf_and_merge.1), channel_id=1, replica_groups=mesh['mesh'=64,'x'=4,'core'=2] {'x'}, dimensions={0} | all-to-all | bytes 1048576 | tf_op jit(solution)/shard_map/all_to_all | solution.py:19
  96.0 2.1 %merge_grams.1 = f32[384,128]{1,0:T(8,128)S(1)} custom-call(bf16[4,512,128]{2,1,0:T(8,128)(2,1)S(1)} %all_to_all.37.bases_ref, bf16[256,128]{1,0:T(8,128)(2,1)} %sketch_ref.5), custom_call_target="tpu_custom_call" | custom-call | tf_op jit(solution)/shard_map/merge_grams/pallas_call | solution.py:347
  98.1 20.4 %all_to_all.38 = f32[128,1,384]{2,1,0:T(1,128)S(1)} all-to-all(f32[128,1,384]{2,1,0:T(1,128)S(1)} %bitcast.16), channel_id=1, replica_groups=mesh['mesh'=64,'x'=4,'core'=2] {'mesh','core'}, dimensions={0} | all-to-all | bytes 393216 | tf_op jit(solution)/shard_map/all_to_all | solution.py:19
  118.5 0.2 reduce_sum.28
  118.7 6.5 %all_to_all.39 = f32[4,1,384]{2,1,0:T(1,128)S(1)} all-to-all(f32[4,1,384]{2,1,0:T(1,128)S(1)} %broadcast_in_dim.18), channel_id=1, replica_groups=mesh['mesh'=64,'x'=4,'core'=2] {'x'}, dimensions={0} | all-to-all | bytes 12288 | tf_op jit(solution)/shard_map/all_to_all | solution.py:19
  125.2 0.1 broadcast_in_dim.19
  125.3 20.3 %all_to_all.40 = f32[128,1,384]{2,1,0:T(1,128)S(1)} all-to-all(f32[128,1,384]{2,1,0:T(1,128)S(1)} %broadcast_in_dim.19), channel_id=1, replica_groups=mesh['mesh'=64,'x'=4,'core'=2] {'mesh','core'}, dimensions={0} | all-to-all | bytes 393216 | tf_op jit(solution)/shard_map/all_to_all | solution.py:19
  145.6 11.7 %last_merges.1 = bf16[128,512]{1,0:T(8,128)(2,1)S(1)} custom-call(f32[384,128]{1,0:T(8,128)S(1)} %bitcast.15, bf16[256,128]{1,0:T(8,128)(2,1)} %sketch_ref.5, bf16[4,512,128]{2,1,0:T(8,128)(2,1)S(1)} %all_to_all.37.bases_ref), custom_call_target="tpu_custom_call" | custom-call | tf_op jit(solution)/shard_map/last_merges/pallas_call | solution.py:351
  157.4 8.0 %all_to_all.41 = bf16[8,16,512]{2,1,0:T(8,128)(2,1)S(1)} all-to-all(bf16[8,16,512]{2,1,0:T(8,128)(2,1)S(1)} %bitcast.17), channel_id=1, replica_groups=mesh['mesh'=64,'x'=4,'core'=2] {'x','core'}, dimensions={0} | all-to-all | bytes 262144 | tf_op jit(solution)/shard_map/all_to_all | solution.py:19
  165.4 0.1 copy.18
  165.5 0.7 reshape.40
  (2 shorter events, 0.0 us)
Async XLA Ops:
  2.0 17.3 %collective-permute-start = (bf16[2448,128]{1,0:T(8,128)(2,1)S(1)}, bf16[2448,128]{1,0:T(8,128)(2,1)S(1)}, u32[]{:S(2)}, u32[]{:S(2)}) collective-permute-start(bf16[2448,128]{1,0:T(8,128)(2,1)S(1)} %get-tuple-element.10), channel_id=1, source_target_pairs={{0,1},{1,0},{2,3},{3,2},{4,5},{5,4},{6,7},{7,6},{8,9},{9,8},{10,11... | collective-permute-start | bytes 1880072 | tf_op jit(solution)/shard_map/ppermute | solution.py:326
  10.7 6.6 %collective-permute-start.1 = (bf16[768,128]{1,0:T(8,128)(2,1)S(1)}, bf16[768,128]{1,0:T(8,128)(2,1)S(1)}, u32[]{:S(2)}, u32[]{:S(2)}) collective-permute-start(bf16[768,128]{1,0:T(8,128)(2,1)S(1)} %get-tuple-element.11), channel_id=1, source_target_pairs={{0,8},{9,1},{8,16},{17,9},{16,24},{25,17},{24,32},{33,25},{32,40},... | collective-permute-start | bytes 589832 | tf_op jit(solution)/shard_map/ppermute | solution.py:324
  12.0 7.2 %collective-permute-start.2 = (bf16[768,128]{1,0:T(8,128)(2,1)S(1)}, bf16[768,128]{1,0:T(8,128)(2,1)S(1)}, u32[]{:S(2)}, u32[]{:S(2)}) collective-permute-start(bf16[768,128]{1,0:T(8,128)(2,1)S(1)} %get-tuple-element.12), channel_id=1, source_target_pairs={{1,8},{8,1},{9,16},{16,9},{17,24},{24,17},{25,32},{32,25},{33,40},... | collective-permute-start | bytes 589832 | tf_op jit(solution)/shard_map/ppermute | solution.py:325
